TPU v7x, 32 devices: a whole 2x2x4 slice. The times are simulated.
32 devices in a mesh: group: 4 (over y, x), slot: 8 (over z, core).
Axes of the slice: x: 2, y: 2, z: 4, core: 2. Of those that a mesh axis runs over, the one named last changes fastest.
Arguments:
- tokens: bfloat16 [4096, 2048], P(('group', 'slot')), may hold values from -6 to 6
- cotangent: bfloat16 [4096, 512], P(('group', 'slot')), may hold values from -0.59765625 to 0.59765625
- weight_halves: bfloat16 [32, 1024, 512], P(('group', 'slot')), may hold values from -0.125 to 0.125
- momentum_halves: bfloat16 [32, 1024, 512], P(('group', 'slot')), may hold values from -6 to 6
- old_map: int32 [4, 4], replicated, may hold values from 0 to 3, each once within a row
- new_map: int32 [4, 8], replicated, may hold values from 0 to 3, as said below
- row_ids: int32 [32, 128], P(('group', 'slot')), may hold values from 0 to 127
Outputs:
- projected: bfloat16 [4096, 512], P(('group', 'slot'))
Inputs may be any that keep to these rules, and one draw needn't show every extreme that they name: `old_map`: each row names each of the group's experts once. `new_map`: every expert is hosted by one to four new slots; among the experts of every owner group one is hosted by exactly four.
All inputs are finite; a program needn't handle non-finite values.
Results may differ from a plain program's by a relative error of at most 0.007.
Values may be sent and summed in bfloat16 or wider, within the bound.
No kernel may reach another device: no remote copies, remote signals or barrier semaphores. Data moves between devices by JAX's collectives and lax.ppermute only.
A program may use at most 64 MiB of HBM per device.

v0:
```python
import math
import jax
import jax.numpy as jnp
from jax import lax
from jax.sharding import PartitionSpec as P

ITERS = 2
coef_a = 3.4445
coef_b = -4.775
coef_c = 2.0315
momentum_rate = 0.95
step_scale = 0.01
gram_eps = 1e-06
contract_rows = (((0,), (0,)), ((), ()))


def swapped(shard, axis, stride):
    return lax.ppermute(shard, axis, [(i, i ^ 1 << stride) for i in range(lax.axis_size(axis))])


def pick_columns(token_block, which_half, slot_count):
    row_count, col_count = token_block.shape
    pieces_view = token_block.reshape(row_count, slot_count, 2, col_count // (2 * slot_count))
    chosen = lax.dynamic_index_in_dim(pieces_view, which_half, axis=2, keepdims=False)
    return chosen.reshape(row_count, col_count // 2)


def inner_gram(half_rows):
    return lax.dot_general(
        half_rows, half_rows, contract_rows, preferred_element_type=jnp.float32
    ).astype(jnp.bfloat16)


def make_polynomial(scaled):
    gram_bf = scaled.astype(jnp.bfloat16)
    square = jnp.dot(gram_bf, gram_bf, preferred_element_type=jnp.float32)
    return (coef_b * scaled + coef_c * square).astype(jnp.bfloat16)


def on_device(tokens, cotangent, weight_halves, momentum_halves, old_map, new_map, row_ids):
    slot_count = lax.axis_size("slot")
    host_count = slot_count // lax.axis_size("group")
    model_width = tokens.shape[1]
    hidden = cotangent.shape[1]
    half_index = lax.axis_index("slot") % 2
    group_id = lax.axis_index("group")
    outgoing = jnp.concatenate(
        [pick_columns(tokens, 1 - half_index, slot_count), cotangent], axis=1
    )
    incoming = swapped(outgoing, "slot", 0)
    own_term = lax.dot_general(
        pick_columns(tokens, half_index, slot_count),
        cotangent,
        contract_rows,
        preferred_element_type=jnp.float32,
    ).astype(jnp.bfloat16)
    peer_term = lax.dot_general(
        incoming[:, : model_width // 2],
        incoming[:, model_width // 2 :],
        contract_rows,
        preferred_element_type=jnp.float32,
    ).astype(jnp.bfloat16)
    gradient = own_term.astype(jnp.float32) + peer_term.astype(jnp.float32)
    current = (momentum_rate * momentum_halves[0].astype(jnp.float32) + gradient).astype(
        jnp.bfloat16
    )
    own_gram = inner_gram(current)
    for iteration in range(ITERS):
        peer_gram = swapped(own_gram, "slot", 0)
        gram_sum = own_gram.astype(jnp.float32) + peer_gram.astype(jnp.float32)
        if iteration == 0:
            norm_sq = jnp.trace(gram_sum) + gram_eps
            gram_sum = gram_sum / norm_sq
            factor = 1.0 / jnp.sqrt(norm_sq)
        else:
            factor = 1.0
        polynomial = make_polynomial(gram_sum)
        product = jnp.dot(current, polynomial, preferred_element_type=jnp.float32)
        current = (factor * (coef_a * current.astype(jnp.float32) + product)).astype(jnp.bfloat16)
        if iteration + 1 < ITERS:
            own_gram = inner_gram(current)
    renewed = (
        weight_halves[0].astype(jnp.float32)
        - step_scale * math.sqrt(model_width) * current.astype(jnp.float32)
    ).astype(jnp.bfloat16)
    blocks = lax.all_to_all(
        renewed.reshape(slot_count, -1, hidden), "slot", split_axis=0, concat_axis=0, tiled=True
    )
    pieces = blocks.reshape(slot_count // 2, -1, hidden)
    requests = lax.dynamic_slice_in_dim(new_map, group_id * host_count, host_count, axis=1).reshape(
        -1
    )
    own_list = lax.dynamic_index_in_dim(old_map, group_id, 0, keepdims=False)
    holder = jnp.argmax((own_list[None, :] == requests[:, None]).astype(jnp.int32), axis=1)
    outgoing_blocks = jnp.take(pieces, holder, axis=0)
    weight_new = lax.all_to_all(
        lax.all_to_all(outgoing_blocks, "group", split_axis=0, concat_axis=0, tiled=True),
        "slot",
        split_axis=0,
        concat_axis=1,
        tiled=True,
    )[0]
    chosen = jnp.take(tokens, row_ids[0], axis=0)
    return jnp.dot(chosen, weight_new, preferred_element_type=jnp.float32).astype(jnp.bfloat16)


def solution(mesh):
    placed = (
        P(("group", "slot"), None),
        P(("group", "slot"), None),
        P(("group", "slot"), None, None),
        P(("group", "slot"), None, None),
        P(),
        P(),
        P(("group", "slot"), None),
    )
    return jax.shard_map(
        on_device, mesh=mesh, in_specs=placed, out_specs=P(("group", "slot"), None), check_vma=False
    )
```

profile of v0, /device:TPU:0, one launch (start us, length us, event | category | flops | bytes accessed | tf_op | source)
XLA Modules:
  0.0 131.6 jit_solution(12882281342114190404)
XLA Ops:
  0.0 0.0 copy-start
  0.0 1.4 %copy.11 = bf16[128,2048]{0,1:T(8,128)(2,1)S(1)} copy(bf16[128,2048]{1,0:T(8,128)(2,1)} %param.7) | data formatting | bytes 1048576 | tf_op args[0]
  1.4 1.0 copy.12
  2.5 0.6 collective-permute-start
  3.1 0.4 convolution_convert_fusion.1
  3.5 0.9 collective-permute-done
  4.5 0.5 fusion.1
  5.0 0.7 convolution_convert_fusion.3
  5.7 0.4 collective-permute-start.1
  6.2 1.5 %collective-permute-done.1 = bf16[512,512]{1,0:T(8,128)(2,1)S(1)} collective-permute-done((bf16[512,512]{1,0:T(8,128)(2,1)S(1)}, bf16[512,512]{1,0:T(8,128)(2,1)S(1)}, u32[]{:S(2)}, u32[]{:S(2)}) %collective-permute-start.1) | collective-permute-done | bytes 524320 | tf_op jit(solution)/shard_map/ppermute | solution.py:18
  7.7 0.7 select_reduce_fusion
  9.1 1.2 multiply_convert_fusion
  10.3 0.0 copy-start.4
  10.3 0.7 convolution_convert_fusion.2
  11.0 0.4 collective-permute-start.2
  11.4 1.5 %collective-permute-done.2 = bf16[512,512]{1,0:T(8,128)(2,1)S(1)} collective-permute-done((bf16[512,512]{1,0:T(8,128)(2,1)S(1)}, bf16[512,512]{1,0:T(8,128)(2,1)S(1)}, u32[]{:S(2)}, u32[]{:S(2)}) %collective-permute-start.2) | collective-permute-done | bytes 524320 | tf_op jit(solution)/shard_map/ppermute | solution.py:18
  13.0 2.3 %fusion = bf16[1024,512]{1,0:T(8,128)(2,1)} fusion(bf16[1024,512]{1,0:T(8,128)(2,1)S(1)} %multiply_convert_fusion, bf16[1,1024,512]{2,1,0:T(8,128)(2,1)S(1)} %copy-done.4, bf16[512,512]{1,0:T(8,128)(2,1)S(1)} %collective-permute-done.2, bf16[512,512]{1,0:T(8,128)(2,1)S(1)} %convolution_convert_fusion.2), kind=kOutput, calls=%fused_computation.3 | convolution fusion | flops 812908544 | bytes 4194304 | tf_op jit(solution)/shard_map/dot_general | solution.py:78
  15.3 6.2 %all-to-all-start = ((bf16[8,128,512]{2,1,0:T(8,128)(2,1)}), bf16[8,128,512]{2,1,0:T(8,128)(2,1)S(1)}, u32[]{:S(2)}, u32[]{:S(2)}) async-start(bf16[8,128,512]{2,1,0:T(8,128)(2,1)} %bitcast.9), calls=%async_computation | async-start | bytes 2097152 | tf_op jit(solution)/shard_map/all_to_all | solution.py:86
  21.5 0.0 copy-done
  21.5 0.1 constant_dynamic-slice_fusion.2
  21.6 0.1 eq.27
  21.7 0.7 fusion.24
  22.3 0.6 iota_reduce_fusion
  23.0 25.1 %all-to-all-done = bf16[8,128,512]{2,1,0:T(8,128)(2,1)S(1)} async-done(((bf16[8,128,512]{2,1,0:T(8,128)(2,1)}), bf16[8,128,512]{2,1,0:T(8,128)(2,1)S(1)}, u32[]{:S(2)}, u32[]{:S(2)}) %all-to-all-start) | async-done | bytes 1048608 | tf_op jit(solution)/shard_map/all_to_all | solution.py:86
  48.0 0.7 gather_fusion.1
  48.7 0.3 broadcast_select_fusion
  49.0 28.7 %all_to_all.19 = bf16[8,256,512]{2,1,0:T(8,128)(2,1)} all-to-all(bf16[8,256,512]{2,1,0:T(8,128)(2,1)S(1)} %broadcast_select_fusion), channel_id=1, replica_groups=mesh['group'=4,'slot'=8] {'group'}, dimensions={0} | all-to-all | bytes 4194304 | tf_op jit(solution)/shard_map/all_to_all | solution.py:97
  77.7 3.7 %all-to-all-start.2 = ((bf16[8,256,512]{2,1,0:T(8,128)(2,1)}), bf16[8,256,512]{2,1,0:T(8,128)(2,1)S(1)}, u32[]{:S(2)}, u32[]{:S(2)}) async-start(bf16[8,256,512]{2,1,0:T(8,128)(2,1)} %all_to_all.19), calls=%async_computation.2 | async-start | bytes 4194304 | tf_op jit(solution)/shard_map/all_to_all | solution.py:96
  81.5 0.0 copy-done.5
  81.5 0.9 gather_fusion
  82.5 48.0 %all-to-all-done.2 = bf16[8,256,512]{2,1,0:T(8,128)(2,1)S(1)} async-done(((bf16[8,256,512]{2,1,0:T(8,128)(2,1)}), bf16[8,256,512]{2,1,0:T(8,128)(2,1)S(1)}, u32[]{:S(2)}, u32[]{:S(2)}) %all-to-all-start.2) | async-done | bytes 2097184 | tf_op jit(solution)/shard_map/all_to_all | solution.py:96
  130.4 1.1 convolution_convert_fusion.4
  (16 shorter events, 0.1 us)
Async XLA Ops:
  0.0 21.5 %copy-start = (s32[4,8]{1,0:T(4,128)S(1)}, s32[4,8]{1,0:T(4,128)}, u32[]{:S(2)}) copy-start(s32[4,8]{1,0:T(4,128)} %param.12) | copy-start | bytes 388
  0.0 3.1 %copy-start.3 = (bf16[128,512]{1,0:T(8,128)(2,1)S(1)}, bf16[128,512]{1,0:T(8,128)(2,1)}, u32[]{:S(2)}) copy-start(bf16[128,512]{1,0:T(8,128)(2,1)} %param.8) | copy-start | bytes 393220
  0.0 4.5 %copy-start.2 = (bf16[1,1024,512]{2,1,0:T(8,128)(2,1)S(1)}, bf16[1,1024,512]{2,1,0:T(8,128)(2,1)}, u32[]{:S(2)}) copy-start(bf16[1,1024,512]{2,1,0:T(8,128)(2,1)} %param.10) | copy-start | bytes 3145732
  2.5 1.9 %collective-permute-start = (bf16[128,1536]{0,1:T(8,128)(2,1)S(1)}, bf16[128,1536]{0,1:T(8,128)(2,1)S(1)}, u32[]{:S(2)}, u32[]{:S(2)}) collective-permute-start(bf16[128,1536]{0,1:T(8,128)(2,1)S(1)} %pad_maximum_fusion), channel_id=1, source_target_pairs={{0,1},{1,0},{2,3},{3,2},{4,5},{5,4},{6,7},{7,6},{8,9},{9,8},{10,11... | collective-permute-start | bytes 1179656 | tf_op jit(solution)/shard_map/ppermute | solution.py:18
  5.7 2.0 %collective-permute-start.1 = (bf16[512,512]{1,0:T(8,128)(2,1)S(1)}, bf16[512,512]{1,0:T(8,128)(2,1)S(1)}, u32[]{:S(2)}, u32[]{:S(2)}) collective-permute-start(bf16[512,512]{1,0:T(8,128)(2,1)S(1)} %convolution_convert_fusion.3), channel_id=1, source_target_pairs={{0,1},{1,0},{2,3},{3,2},{4,5},{5,4},{6,7},{7,6},{8,9},{9,8},{10,11... | collective-permute-start | bytes 1572872 | tf_op jit(solution)/shard_map/ppermute | solution.py:18
  10.3 2.7 %copy-start.4 = (bf16[1,1024,512]{2,1,0:T(8,128)(2,1)S(1)}, bf16[1,1024,512]{2,1,0:T(8,128)(2,1)}, u32[]{:S(2)}) copy-start(bf16[1,1024,512]{2,1,0:T(8,128)(2,1)} %param.9) | copy-start | bytes 3145732
  11.0 2.0 %collective-permute-start.2 = (bf16[512,512]{1,0:T(8,128)(2,1)S(1)}, bf16[512,512]{1,0:T(8,128)(2,1)S(1)}, u32[]{:S(2)}, u32[]{:S(2)}) collective-permute-start(bf16[512,512]{1,0:T(8,128)(2,1)S(1)} %convolution_convert_fusion.2), channel_id=1, source_target_pairs={{0,1},{1,0},{2,3},{3,2},{4,5},{5,4},{6,7},{7,6},{8,9},{9,8},{10,11... | collective-permute-start | bytes 1572872 | tf_op jit(solution)/shard_map/ppermute | solution.py:18
  15.3 32.8 %all-to-all-start = ((bf16[8,128,512]{2,1,0:T(8,128)(2,1)}), bf16[8,128,512]{2,1,0:T(8,128)(2,1)S(1)}, u32[]{:S(2)}, u32[]{:S(2)}) async-start(bf16[8,128,512]{2,1,0:T(8,128)(2,1)} %bitcast.9), calls=%async_computation | async-start | bytes 2097152 | tf_op jit(solution)/shard_map/all_to_all | solution.py:86
  77.7 3.7 %copy-start.5 = (s32[1,128]{1,0:T(1,128)S(1)}, s32[1,128]{1,0:T(1,128)}, u32[]{:S(2)}) copy-start(s32[1,128]{1,0:T(1,128)} %param.13) | copy-start | bytes 1540
  77.7 3.8 %copy-start.1 = (bf16[128,2048]{1,0:T(8,128)(2,1)S(1)}, bf16[128,2048]{1,0:T(8,128)(2,1)}, u32[]{:S(2)}) copy-start(bf16[128,2048]{1,0:T(8,128)(2,1)} %param.7) | copy-start | bytes 1572868
  77.7 52.7 %all-to-all-start.2 = ((bf16[8,256,512]{2,1,0:T(8,128)(2,1)}), bf16[8,256,512]{2,1,0:T(8,128)(2,1)S(1)}, u32[]{:S(2)}, u32[]{:S(2)}) async-start(bf16[8,256,512]{2,1,0:T(8,128)(2,1)} %all_to_all.19), calls=%async_computation.2 | async-start | bytes 4194304 | tf_op jit(solution)/shard_map/all_to_all | solution.py:96
where the time goes:
time: 132 us
  waiting for transfers between devices  77.1 us (58%)
  blocking collectives  28.7 us (22%)
  starting transfers between devices  11.4 us (9%)
  matrix products  7.01 us (5%)
  local copies, waits for them, and re-layouts  4.96 us (4%)
  other arithmetic  1.6 us (1%)
    all_to_all x1, waiting for transfers between devices, on_device(): lax.all_to_all(lax.all_to_all(outgoing_blocks, 'group', split_axis=0, con...  48 us
    all_to_all x1, blocking collectives, on_device(): lax.all_to_all(outgoing_blocks, 'group', split_axis=0, concat_axis=0, til...  28.7 us
    all_to_all x1, waiting for transfers between devices, on_device(): lax.all_to_all(renewed.reshape(slot_count, -1, hidden), 'slot', split_axi...  25.1 us
    all_to_all x1, starting transfers between devices, on_device(): lax.all_to_all(renewed.reshape(slot_count, -1, hidden), 'slot', split_axi...  6.22 us
    ppermute x3, waiting for transfers between devices, swapped(): lax.ppermute(shard, axis, [(i, i ^ 1 << stride) for i in range(lax.axis_s...  4.01 us
    all_to_all x1, starting transfers between devices, on_device(): lax.all_to_all(lax.all_to_all(outgoing_blocks, 'group', split_axis=0, con...  3.73 us
    dot_general x2, matrix products, on_device(): product = jnp.dot(current, polynomial, preferred_element_type=jnp.float32)  3.44 us
  transfers between devices with their start and end apart: 5, of which 5 were waited for; matrix products, arithmetic and copies ran while one was open for 2% of the time, Pallas kernels for 0%

commit v1 on v0

--- a/solution.py
+++ b/solution.py
@@ -83,9 +83,16 @@
         weight_halves[0].astype(jnp.float32)
         - step_scale * math.sqrt(model_width) * current.astype(jnp.float32)
     ).astype(jnp.bfloat16)
-    blocks = lax.all_to_all(
-        renewed.reshape(slot_count, -1, hidden), "slot", split_axis=0, concat_axis=0, tiled=True
-    )
+    x = renewed.reshape(slot_count, -1, hidden)
+    ways, here = (lax.axis_size("slot"), lax.axis_index("slot"))
+    width = x.shape[0] // ways
+    turned = jnp.roll(x, -here * width, axis=0)
+    got = [lax.slice_in_dim(turned, 0, width, axis=0)]
+    for far in range(1, ways):
+        sent = lax.slice_in_dim(turned, far * width, (far + 1) * width, axis=0)
+        got.append(lax.ppermute(sent, "slot", [(d, (d + far) % ways) for d in range(ways)]))
+    line = jnp.concatenate(got[::-1], axis=0)
+    blocks = jnp.roll(line, (here + 1) * got[0].shape[0], axis=0)
     pieces = blocks.reshape(slot_count // 2, -1, hidden)
     requests = lax.dynamic_slice_in_dim(new_map, group_id * host_count, host_count, axis=1).reshape(
         -1

time: 132 us -> 129 us (0.977)
  waiting for transfers between devices: 77.1 us -> 70.9 us
  starting transfers between devices: 11.4 us -> 14 us
    all_to_all x1 -> x0, waiting for transfers between devices: 25.1 us -> none  [on_device(): lax.all_to_all(renewed.reshape(slot_count, -1, hidden), 'slot', split_axi...]
    ppermute x0 -> x7, waiting for transfers between devices: none -> 20.2 us  [on_device(): lax.ppermute(sent, 'slot', [(d, (d + far) % ways) for d in range(ways)])]
    ppermute x0 -> x7, starting transfers between devices: none -> 7.77 us  [on_device(): lax.ppermute(sent, 'slot', [(d, (d + far) % ways) for d in range(ways)])]
    all_to_all x1 -> x0, starting transfers between devices: 6.22 us -> none  [on_device(): lax.all_to_all(renewed.reshape(slot_count, -1, hidden), 'slot', split_axi...]
    all_to_all x1, blocking collectives: 28.7 us -> 27.4 us  [on_device(): lax.all_to_all(outgoing_blocks, 'group', split_axis=0, concat_axis=0, til...]
    ppermute x3, waiting for transfers between devices: 4.01 us -> 2.69 us  [swapped(): lax.ppermute(shard, axis, [(i, i ^ 1 << stride) for i in range(lax.axis_s...]
    unnamed x14 -> x23, local copies, waits for them, and re-layouts: 2.46 us -> 2.73 us
  transfers between devices with their start and end apart: 5 -> 11, of which waited for: 5 -> 9; matrix products, arithmetic and copies ran while one was open for 2% -> 2% of each run, Pallas kernels for 0% -> 0%
where the time goes in v1:
time: 129 us
  waiting for transfers between devices  70.9 us (55%)
  blocking collectives  27.4 us (21%)
  starting transfers between devices  14 us (11%)
  matrix products  8.16 us (6%)
  local copies, waits for them, and re-layouts  5.33 us (4%)
  other arithmetic  2.38 us (2%)
    all_to_all x1, waiting for transfers between devices, on_device(): lax.all_to_all(lax.all_to_all(outgoing_blocks, 'group', split_axis=0, con...  48 us
    all_to_all x1, blocking collectives, on_device(): lax.all_to_all(outgoing_blocks, 'group', split_axis=0, concat_axis=0, til...  27.4 us
    ppermute x7, waiting for transfers between devices, on_device(): lax.ppermute(sent, 'slot', [(d, (d + far) % ways) for d in range(ways)])  20.2 us
    ppermute x7, starting transfers between devices, on_device(): lax.ppermute(sent, 'slot', [(d, (d + far) % ways) for d in range(ways)])  7.77 us
    all_to_all x1, starting transfers between devices, on_device(): lax.all_to_all(lax.all_to_all(outgoing_blocks, 'group', split_axis=0, con...  4.86 us
    dot_general x2, matrix products, on_device(): product = jnp.dot(current, polynomial, preferred_element_type=jnp.float32)  4.59 us
    unnamed x23, local copies, waits for them, and re-layouts  2.73 us
    ppermute x3, waiting for transfers between devices, swapped(): lax.ppermute(shard, axis, [(i, i ^ 1 << stride) for i in range(lax.axis_s...  2.69 us
  transfers between devices with their start and end apart: 11, of which 9 were waited for; matrix products, arithmetic and copies ran while one was open for 2% of the time, Pallas kernels for 0%

profile of v1, /device:TPU:0, one launch (start us, length us, event | category | flops | bytes accessed | tf_op | source)
XLA Modules:
  0.0 129.1 jit_solution(6221473847338357246)
XLA Ops:
  0.0 1.4 %copy.11 = bf16[128,2048]{0,1:T(8,128)(2,1)S(1)} copy(bf16[128,2048]{1,0:T(8,128)(2,1)} %param.9) | data formatting | bytes 1048576 | tf_op args[0]
  1.4 1.0 copy.12
  2.6 0.6 collective-permute-start
  3.1 0.4 convolution_convert_fusion.1
  3.5 0.9 collective-permute-done
  4.5 0.5 fusion.1
  5.0 0.7 convolution_convert_fusion.3
  5.8 0.4 collective-permute-start.1
  6.4 1.4 %collective-permute-done.1 = bf16[512,512]{1,0:T(8,128)(2,1)S(1)} collective-permute-done((bf16[512,512]{1,0:T(8,128)(2,1)S(1)}, bf16[512,512]{1,0:T(8,128)(2,1)S(1)}, u32[]{:S(2)}, u32[]{:S(2)}) %collective-permute-start.1) | collective-permute-done | bytes 524320 | tf_op jit(solution)/shard_map/ppermute | solution.py:18
  7.7 0.7 select_reduce_fusion
  9.1 1.2 multiply_convert_fusion
  10.3 0.7 convolution_convert_fusion.2
  11.6 0.7 fusion.26
  12.3 0.6 iota_reduce_fusion
  12.9 0.4 collective-permute-done.2
  13.3 3.4 %fusion = bf16[1024,512]{1,0:T(8,128)(2,1)S(1)} fusion(bf16[1024,512]{1,0:T(8,128)(2,1)} %copy-done.6, bf16[1,1024,512]{2,1,0:T(8,128)(2,1)S(1)} %copy-done.4, bf16[512,512]{1,0:T(8,128)(2,1)} %collective-permute-done.2, bf16[512,512]{1,0:T(8,128)(2,1)S(1)} %convolution_convert_fusion.2), kind=kOutput, calls=%fused_computation.7 | convolution fusion | flops 812908544 | bytes 4194304 | tf_op jit(solution)/shard_map/dot_general | solution.py:78
  16.7 0.4 fusion.3
  17.2 4.8 %collective-permute-start.3 = (bf16[1,128,512]{2,1,0:T(8,128)(2,1)S(1)}, bf16[1,128,512]{2,1,0:T(8,128)(2,1)S(1)}, u32[]{:S(2)}, u32[]{:S(2)}) collective-permute-start(bf16[1,128,512]{2,1,0:T(8,128)(2,1)S(1)} %get-tuple-element.14), channel_id=1, source_target_pairs={{0,7},{1,0},{2,1},{3,2},{4,3},{5,4},{6,5},{7,6},{8,15},{9,8},{10,9... | collective-permute-start | bytes 393224 | tf_op jit(solution)/shard_map/ppermute | solution.py:93
  22.0 0.4 collective-permute-start.4
  22.4 2.6 %collective-permute-start.6 = (bf16[1,128,512]{2,1,0:T(8,128)(2,1)S(1)}, bf16[1,128,512]{2,1,0:T(8,128)(2,1)S(1)}, u32[]{:S(2)}, u32[]{:S(2)}) collective-permute-start(bf16[1,128,512]{2,1,0:T(8,128)(2,1)S(1)} %get-tuple-element.11), channel_id=1, source_target_pairs={{0,4},{1,5},{2,6},{3,7},{4,0},{5,1},{6,2},{7,3},{8,12},{9,13},{10,... | collective-permute-start | bytes 393224 | tf_op jit(solution)/shard_map/ppermute | solution.py:93
  25.0 0.9 collective-permute-done.3
  25.9 3.0 %collective-permute-done.4 = bf16[1,128,512]{2,1,0:T(8,128)(2,1)S(1)} collective-permute-done((bf16[1,128,512]{2,1,0:T(8,128)(2,1)S(1)}, bf16[1,128,512]{2,1,0:T(8,128)(2,1)S(1)}, u32[]{:S(2)}, u32[]{:S(2)}) %collective-permute-start.4) | collective-permute-done | bytes 131104 | tf_op jit(solution)/shard_map/ppermute | solution.py:93
  29.0 2.6 %collective-permute-done.5 = bf16[1,128,512]{2,1,0:T(8,128)(2,1)S(1)} collective-permute-done((bf16[1,128,512]{2,1,0:T(8,128)(2,1)S(1)}, bf16[1,128,512]{2,1,0:T(8,128)(2,1)S(1)}, u32[]{:S(2)}, u32[]{:S(2)}) %collective-permute-start.5) | collective-permute-done | bytes 131104 | tf_op jit(solution)/shard_map/ppermute | solution.py:93
  31.6 12.8 %collective-permute-done.6 = bf16[1,128,512]{2,1,0:T(8,128)(2,1)S(1)} collective-permute-done((bf16[1,128,512]{2,1,0:T(8,128)(2,1)S(1)}, bf16[1,128,512]{2,1,0:T(8,128)(2,1)S(1)}, u32[]{:S(2)}, u32[]{:S(2)}) %collective-permute-start.6) | collective-permute-done | bytes 131104 | tf_op jit(solution)/shard_map/ppermute | solution.py:93
  44.3 0.9 collective-permute-done.7
  45.3 0.4 fusion.2
  45.7 0.7 gather_fusion.1
  46.7 27.4 %all_to_all.14 = bf16[8,256,512]{2,1,0:T(8,128)(2,1)} all-to-all(bf16[8,256,512]{2,1,0:T(8,128)(2,1)S(1)} %broadcast_select_fusion), channel_id=1, replica_groups=mesh['group'=4,'slot'=8] {'group'}, dimensions={0} | all-to-all | bytes 4194304 | tf_op jit(solution)/shard_map/all_to_all | solution.py:104
  74.0 4.9 %all-to-all-start.1 = ((bf16[8,256,512]{2,1,0:T(8,128)(2,1)}), bf16[8,256,512]{2,1,0:T(8,128)(2,1)S(1)}, u32[]{:S(2)}, u32[]{:S(2)}) async-start(bf16[8,256,512]{2,1,0:T(8,128)(2,1)} %all_to_all.14), calls=%async_computation.1 | async-start | bytes 4194304 | tf_op jit(solution)/shard_map/all_to_all | solution.py:103
  78.9 0.9 gather_fusion
  79.9 48.0 %all-to-all-done.1 = bf16[8,256,512]{2,1,0:T(8,128)(2,1)S(1)} async-done(((bf16[8,256,512]{2,1,0:T(8,128)(2,1)}), bf16[8,256,512]{2,1,0:T(8,128)(2,1)S(1)}, u32[]{:S(2)}, u32[]{:S(2)}) %all-to-all-start.1) | async-done | bytes 2097184 | tf_op jit(solution)/shard_map/all_to_all | solution.py:103
  127.9 1.2 convolution_convert_fusion.4
  (41 shorter events, 1.3 us)
Async XLA Ops:
  0.0 6.2 %copy-start = (s32[4,8]{1,0:T(4,128)S(1)}, s32[4,8]{1,0:T(4,128)}, u32[]{:S(2)}) copy-start(s32[4,8]{1,0:T(4,128)} %param.14) | copy-start | bytes 388
  0.0 3.1 %copy-start.3 = (bf16[128,512]{1,0:T(8,128)(2,1)S(1)}, bf16[128,512]{1,0:T(8,128)(2,1)}, u32[]{:S(2)}) copy-start(bf16[128,512]{1,0:T(8,128)(2,1)} %param.10) | copy-start | bytes 393220
  0.0 4.5 %copy-start.2 = (bf16[1,1024,512]{2,1,0:T(8,128)(2,1)S(1)}, bf16[1,1024,512]{2,1,0:T(8,128)(2,1)}, u32[]{:S(2)}) copy-start(bf16[1,1024,512]{2,1,0:T(8,128)(2,1)} %param.12) | copy-start | bytes 3145732
  2.6 1.9 %collective-permute-start = (bf16[128,1536]{0,1:T(8,128)(2,1)S(1)}, bf16[128,1536]{0,1:T(8,128)(2,1)S(1)}, u32[]{:S(2)}, u32[]{:S(2)}) collective-permute-start(bf16[128,1536]{0,1:T(8,128)(2,1)S(1)} %pad_maximum_fusion), channel_id=1, source_target_pairs={{0,1},{1,0},{2,3},{3,2},{4,5},{5,4},{6,7},{7,6},{8,9},{9,8},{10,11... | collective-permute-start | bytes 1179656 | tf_op jit(solution)/shard_map/ppermute | solution.py:18
  5.8 2.0 %collective-permute-start.1 = (bf16[512,512]{1,0:T(8,128)(2,1)S(1)}, bf16[512,512]{1,0:T(8,128)(2,1)S(1)}, u32[]{:S(2)}, u32[]{:S(2)}) collective-permute-start(bf16[512,512]{1,0:T(8,128)(2,1)S(1)} %convolution_convert_fusion.3), channel_id=1, source_target_pairs={{0,1},{1,0},{2,3},{3,2},{4,5},{5,4},{6,7},{7,6},{8,9},{9,8},{10,11... | collective-permute-start | bytes 1572872 | tf_op jit(solution)/shard_map/ppermute | solution.py:18
  10.3 1.0 copy-start.6
  10.3 3.0 %copy-start.4 = (bf16[1,1024,512]{2,1,0:T(8,128)(2,1)S(1)}, bf16[1,1024,512]{2,1,0:T(8,128)(2,1)}, u32[]{:S(2)}) copy-start(bf16[1,1024,512]{2,1,0:T(8,128)(2,1)} %param.11) | copy-start | bytes 3145732
  11.2 2.0 %collective-permute-start.2 = (bf16[512,512]{1,0:T(8,128)(2,1)S(1)}, bf16[512,512]{1,0:T(8,128)(2,1)}, u32[]{:S(2)}, u32[]{:S(2)}) collective-permute-start(bf16[512,512]{1,0:T(8,128)(2,1)S(1)} %convolution_convert_fusion.2), channel_id=1, source_target_pairs={{0,1},{1,0},{2,3},{3,2},{4,5},{5,4},{6,7},{7,6},{8,9},{9,8},{10,11... | collective-permute-start | bytes 1572872 | tf_op jit(solution)/shard_map/ppermute | solution.py:18
  17.2 8.7 %collective-permute-start.3 = (bf16[1,128,512]{2,1,0:T(8,128)(2,1)S(1)}, bf16[1,128,512]{2,1,0:T(8,128)(2,1)S(1)}, u32[]{:S(2)}, u32[]{:S(2)}) collective-permute-start(bf16[1,128,512]{2,1,0:T(8,128)(2,1)S(1)} %get-tuple-element.14), channel_id=1, source_target_pairs={{0,7},{1,0},{2,1},{3,2},{4,3},{5,4},{6,5},{7,6},{8,15},{9,8},{10,9... | collective-permute-start | bytes 393224 | tf_op jit(solution)/shard_map/ppermute | solution.py:93
  22.0 7.0 %collective-permute-start.4 = (bf16[1,128,512]{2,1,0:T(8,128)(2,1)S(1)}, bf16[1,128,512]{2,1,0:T(8,128)(2,1)S(1)}, u32[]{:S(2)}, u32[]{:S(2)}) collective-permute-start(bf16[1,128,512]{2,1,0:T(8,128)(2,1)S(1)} %get-tuple-element.13), channel_id=1, source_target_pairs={{0,6},{1,7},{2,0},{3,1},{4,2},{5,3},{6,4},{7,5},{8,14},{9,15},{10,... | collective-permute-start | bytes 393224 | tf_op jit(solution)/shard_map/ppermute | solution.py:93
  22.4 9.1 %collective-permute-start.5 = (bf16[1,128,512]{2,1,0:T(8,128)(2,1)S(1)}, bf16[1,128,512]{2,1,0:T(8,128)(2,1)S(1)}, u32[]{:S(2)}, u32[]{:S(2)}) collective-permute-start(bf16[1,128,512]{2,1,0:T(8,128)(2,1)S(1)} %get-tuple-element.12), channel_id=1, source_target_pairs={{0,5},{1,6},{2,7},{3,0},{4,1},{5,2},{6,3},{7,4},{8,13},{9,14},{10,... | collective-permute-start | bytes 393224 | tf_op jit(solution)/shard_map/ppermute | solution.py:93
  22.4 21.9 %collective-permute-start.6 = (bf16[1,128,512]{2,1,0:T(8,128)(2,1)S(1)}, bf16[1,128,512]{2,1,0:T(8,128)(2,1)S(1)}, u32[]{:S(2)}, u32[]{:S(2)}) collective-permute-start(bf16[1,128,512]{2,1,0:T(8,128)(2,1)S(1)} %get-tuple-element.11), channel_id=1, source_target_pairs={{0,4},{1,5},{2,6},{3,7},{4,0},{5,1},{6,2},{7,3},{8,12},{9,13},{10,... | collective-permute-start | bytes 393224 | tf_op jit(solution)/shard_map/ppermute | solution.py:93
  25.0 20.2 %collective-permute-start.7 = (bf16[1,128,512]{2,1,0:T(8,128)(2,1)S(1)}, bf16[1,128,512]{2,1,0:T(8,128)(2,1)S(1)}, u32[]{:S(2)}, u32[]{:S(2)}) collective-permute-start(bf16[1,128,512]{2,1,0:T(8,128)(2,1)S(1)} %get-tuple-element.10), channel_id=1, source_target_pairs={{0,3},{1,4},{2,5},{3,6},{4,7},{5,0},{6,1},{7,2},{8,11},{9,12},{10,... | collective-permute-start | bytes 393224 | tf_op jit(solution)/shard_map/ppermute | solution.py:93
  25.9 19.3 %collective-permute-start.8 = (bf16[1,128,512]{2,1,0:T(8,128)(2,1)S(1)}, bf16[1,128,512]{2,1,0:T(8,128)(2,1)S(1)}, u32[]{:S(2)}, u32[]{:S(2)}) collective-permute-start(bf16[1,128,512]{2,1,0:T(8,128)(2,1)S(1)} %get-tuple-element.9), channel_id=1, source_target_pairs={{0,2},{1,3},{2,4},{3,5},{4,6},{5,7},{6,0},{7,1},{8,10},{9,11},{10,... | collective-permute-start | bytes 393224 | tf_op jit(solution)/shard_map/ppermute | solution.py:93
  28.9 16.3 %collective-permute-start.9 = (bf16[1,128,512]{2,1,0:T(8,128)(2,1)S(1)}, bf16[1,128,512]{2,1,0:T(8,128)(2,1)S(1)}, u32[]{:S(2)}, u32[]{:S(2)}) collective-permute-start(bf16[1,128,512]{2,1,0:T(8,128)(2,1)S(1)} %get-tuple-element.8), channel_id=1, source_target_pairs={{0,1},{1,2},{2,3},{3,4},{4,5},{5,6},{6,7},{7,0},{8,9},{9,10},{10,1... | collective-permute-start | bytes 393224 | tf_op jit(solution)/shard_map/ppermute | solution.py:93
  74.0 4.9 %copy-start.5 = (s32[1,128]{1,0:T(1,128)S(1)}, s32[1,128]{1,0:T(1,128)}, u32[]{:S(2)}) copy-start(s32[1,128]{1,0:T(1,128)} %param.15) | copy-start | bytes 1540
  74.0 4.9 %copy-start.1 = (bf16[128,2048]{1,0:T(8,128)(2,1)S(1)}, bf16[128,2048]{1,0:T(8,128)(2,1)}, u32[]{:S(2)}) copy-start(bf16[128,2048]{1,0:T(8,128)(2,1)} %param.9) | copy-start | bytes 1572868
  74.0 53.9 %all-to-all-start.1 = ((bf16[8,256,512]{2,1,0:T(8,128)(2,1)}), bf16[8,256,512]{2,1,0:T(8,128)(2,1)S(1)}, u32[]{:S(2)}, u32[]{:S(2)}) async-start(bf16[8,256,512]{2,1,0:T(8,128)(2,1)} %all_to_all.14), calls=%async_computation.1 | async-start | bytes 4194304 | tf_op jit(solution)/shard_map/all_to_all | solution.py:103
